TPU v7x, 32 devices: a whole 2x2x4 slice. The times are simulated.
32 devices in a mesh: section: 4 (over x, core), tp: 8 (over z, y).
Axes of the slice: x: 2, y: 2, z: 4, core: 2. Of those that a mesh axis runs over, the one named last changes fastest.
Arguments:
- layer_inputs: bfloat16 [8, 512, 4096], P('section', None, 'tp'), may hold values from -6 to 6
- weights: bfloat16 [8, 4096, 4096], P('section', 'tp'), may hold values from -0.046875 to 0.046875
- input_basis: bfloat16 [8, 4096, 64], P('section', 'tp'), may hold values from -0.09375 to 0.09375
- output_basis: bfloat16 [8, 4096, 32], P('section', 'tp'), may hold values from -0.09375 to 0.09375
- queries: bfloat16 [8, 512, 2048], P('section', 'tp'), may hold values from -0.00390625 to 0.00390625
- top_cotangent: bfloat16 [512, 4096], replicated, may hold values from -6 to 6
- sequence_example: int32 [4], replicated, may hold values from 0 to 1
Outputs:
- scores: float32 [2, 512], P(None, 'tp')
All inputs are finite; a program needn't handle non-finite values.
Results may differ from a plain program's by a relative error of at most 0.0094.
Values may be sent and summed in bfloat16 or wider, within the bound.
A program may use at most 64 MiB of HBM per device.

v0:
```python
import functools

import jax
import jax.numpy as jnp
from jax import lax
from jax.experimental import pallas as pl
from jax.experimental.pallas import tpu as pltpu
from jax.sharding import PartitionSpec as P

EXAMPLES = 2
AHEAD = 4
MESH = pl.DeviceIdType.MESH
NT = (((1,), (1,)), ((), ()))


def grid_of(tp_count):
    ny = 1
    while (2 * ny) * (2 * ny) <= tp_count:
        ny *= 2
    return tp_count // ny, ny


def slope_of(hidden):
    floats = hidden.astype(jnp.float32)
    logistic = jax.nn.sigmoid(floats)
    return logistic * (1.0 + floats * (1.0 - logistic))


def chain_kernel(
    sections, tp_count, top_ref, w_ref, h_ref, ib_ref, ob_ref, q_ref, se_ref, score_ref,
    buf_u, buf_m, buf_l, w_v, ob_v, ib_v, out_v, part_in, got_in, full_in, grad_v, sum_v, score_v,
    w_sem, recv_u, recv_m, send_m, send_my, relay_u, relay_m, send_l,
    part_send, part_recv, full_send, full_recv, grad_send, grad_recv, score_send, score_recv, credit,
):
    nz, ny = grid_of(tp_count)
    sec = lax.axis_index("section")
    tp = lax.axis_index("tp")
    z, y = tp // ny, lax.rem(tp, ny)
    micro, _, rows, width = buf_u.shape
    is_top = sec == sections - 1
    has_lower = sec > 0

    far = [z]
    for k in range(nz - 1):
        down = nz - 1 - k
        from_low = down - (z >= down).astype(jnp.int32)
        from_high = k + (z <= k).astype(jnp.int32)
        far.append(jnp.where(z < nz // 2, from_low, from_high))
    near = far[:1] + far[:0:-1]

    def peer_z(step):
        return far[step] * ny + y

    def peer_y(step):
        return z * ny + lax.rem(y + step, ny)

    def src_at(zstep, ystep):
        return near[zstep] * ny + lax.rem(y + ystep, ny)

    def w_copy(layer):
        return pltpu.make_async_copy(w_ref.at[layer], w_v.at[layer], w_sem.at[layer])

    def top_copy(m, k):
        return pltpu.make_async_copy(
            top_ref.at[pl.ds(pl.multiple_of(m * rows, rows), rows), pl.ds(k * width, width)],
            buf_u.at[m, k], recv_u.at[m, k])

    def remote(src, dst, ssem, rsem, to_sec, to_tp):
        return pltpu.make_async_remote_copy(
            src_ref=src, dst_ref=dst, send_sem=ssem, recv_sem=rsem,
            device_id=(to_sec, to_tp), device_id_type=MESH)

    rank_in, rank_out = ib_ref.shape[1], ob_ref.shape[1]

    def prepare_bases():
        gap_in = jnp.zeros((rank_in, width), jnp.float32)
        gap_out = jnp.zeros((EXAMPLES * rank_out, width), jnp.float32)
        for layer in range(2):
            basis_in = ib_ref[layer].astype(jnp.float32)
            basis_out = [ob_ref[layer].astype(jnp.float32)] * EXAMPLES
            ins = [basis_in, gap_in] if layer == 0 else [gap_in, basis_in]
            outs = basis_out + [gap_out] if layer == 0 else [gap_out] + basis_out
            ib_v[layer] = jnp.concatenate(ins, 0).astype(jnp.bfloat16)
            ob_v[layer] = jnp.concatenate(outs, 0).astype(jnp.bfloat16)

    @pl.when(is_top)
    def _():
        @pl.loop(0, micro)
        def _(m):
            for k in range(tp_count):
                top_copy(m, k).start()

    w_copy(1).start()
    w_copy(0).start()

    barrier = pltpu.get_barrier_semaphore()

    def greet(to_sec, to_tp):
        pl.semaphore_signal(barrier, inc=1, device_id=(to_sec, to_tp), device_id_type=MESH)

    for step in range(1, tp_count):
        greet(sec, lax.rem(tp + step, tp_count))

    @pl.when(has_lower)
    def _():
        for step in range(nz):
            greet(sec - 1, peer_z(step))

    @pl.when(jnp.logical_not(is_top))
    def _():
        for step in range(nz):
            greet(sec + 1, peer_z(step))

    for step in range(1, sections):
        other = lax.rem(sec + step, sections)

        @pl.when(jnp.logical_and(other != sec + 1, other != sec - 1))
        def _(other=other):
            greet(other, tp)

    prepare_bases()
    linked = has_lower.astype(jnp.int32) + jnp.logical_not(is_top).astype(jnp.int32)
    pl.semaphore_wait(barrier, tp_count + sections - 2 + (nz - 1) * linked)

    def relay_u_copy(m, zstep, ystep):
        src = src_at(zstep, 0)
        return remote(buf_u.at[m, src], buf_u.at[m, src], relay_u.at[m, zstep, ystep],
                      recv_u.at[m, src], sec, peer_y(ystep))

    def relay_m_copy(m, zstep, ystep):
        src = src_at(zstep, 0)
        return remote(buf_m.at[m, src], buf_m.at[m, src], relay_m.at[m, zstep, ystep],
                      recv_m.at[m, src], sec, peer_y(ystep))

    def middle_copy(m, zstep):
        return remote(buf_m.at[m, tp], buf_m.at[m, tp], send_m.at[m, zstep],
                      recv_m.at[m, tp], sec, peer_z(zstep))

    def lower_copy(m, zstep):
        return remote(buf_l.at[m], buf_u.at[m, tp], send_l.at[m, zstep],
                      recv_u.at[m, tp], sec - 1, peer_z(zstep))

    def await_u(m, src):
        remote(buf_u.at[m, src], buf_u.at[m, src], send_my, recv_u.at[m, src], sec, tp).wait_recv()

    def await_m(m, src):
        remote(buf_m.at[m, src], buf_m.at[m, src], send_my, recv_m.at[m, src], sec, tp).wait_recv()

    def product(buf, m, layer, ystep, total=None):
        for zstep in range(nz):
            src = src_at(zstep, ystep)
            columns = pl.ds(pl.multiple_of(src * width, width), width)
            term = lax.dot_general(
                buf[m, src], w_v[layer, :, columns], NT, preferred_element_type=jnp.float32)
            total = term if total is None else total + term
        return total

    def upper(m):
        at = pl.ds(pl.multiple_of(m * rows, rows), rows)
        own = buf_u[m, tp]
        floats = own.astype(jnp.float32)
        slope = slope_of(h_ref[1, at, :])
        total = product(buf_u, m, 1, 0)
        for ystep in range(1, ny):
            @pl.when(jnp.logical_not(is_top))
            def _(ystep=ystep):
                for zstep in range(nz):
                    await_u(m, src_at(zstep, ystep))

            total = product(buf_u, m, 1, ystep, total)
        middle = (floats + slope * total).astype(jnp.bfloat16)
        buf_m[m, tp] = middle

        @pl.when(has_lower)
        def _():
            for step in range(1, nz):
                middle_copy(m, step).start()
            for step in range(1, ny):
                relay_m_copy(m, 0, step).start()

        feats = lax.dot_general(
            own, ob_v[1], NT, preferred_element_type=jnp.float32
        ) + lax.dot_general(middle, ob_v[0], NT, preferred_element_type=jnp.float32)
        example = se_ref[m * rows // (micro * rows // se_ref.shape[0])]
        lane_example = lax.rem(
            lax.broadcasted_iota(jnp.int32, feats.shape, 1) // rank_out, EXAMPLES)
        out_v[at, :] = jnp.where(lane_example == example, feats, 0.0)

    def lower(m):
        at = pl.ds(pl.multiple_of(m * rows, rows), rows)
        floats = buf_m[m, tp].astype(jnp.float32)
        slope = slope_of(h_ref[0, at, :])
        total = product(buf_m, m, 0, 0)
        for ystep in range(1, ny):
            for zstep in range(nz):
                await_m(m, src_at(zstep, ystep))
            total = product(buf_m, m, 0, ystep, total)
        buf_l[m] = (floats + slope * total).astype(jnp.bfloat16)
        for step in [*range(1, nz), 0]:
            lower_copy(m, step).start()

    def tp_copy(src, dst, ssem, rsem, to_tp):
        return remote(src, dst, ssem, rsem, sec, to_tp)

    def part_copy(step):
        to = lax.rem(tp + step, tp_count)
        return tp_copy(part_in.at[to], got_in.at[tp], part_send.at[step], part_recv.at[tp], to)

    def full_copy(step):
        to = lax.rem(tp + step, tp_count)
        return tp_copy(full_in.at[tp], full_in.at[tp], full_send.at[step], full_recv.at[tp], to)

    def grad_copy(step):
        to = lax.rem(tp + step, tp_count)
        return tp_copy(grad_v.at[tp], grad_v.at[tp], grad_send.at[step], grad_recv.at[tp], to)

    def score_copy(step):
        to = lax.rem(sec + step, sections)
        return remote(score_v.at[sec], score_v.at[sec], score_send.at[step],
                      score_recv.at[sec], to, tp)

    def project_inputs():
        part_rows = part_in.shape[1]

        @pl.loop(0, tp_count)
        def _(k):
            at = pl.ds(pl.multiple_of(k * part_rows, part_rows), part_rows)
            total = None
            for layer in range(2):
                floats = h_ref[layer, at, :].astype(jnp.float32)
                activated = (floats * jax.nn.sigmoid(floats)).astype(jnp.bfloat16)
                term = lax.dot_general(
                    activated, ib_v[layer], NT, preferred_element_type=jnp.float32)
                total = term if total is None else total + term
            part_in[k] = total

        for step in range(1, tp_count):
            part_copy(step).start()
        total = part_in[tp]
        for step in range(1, tp_count):
            src = lax.rem(tp + step, tp_count)
            tp_copy(got_in.at[src], got_in.at[src], send_my, part_recv.at[src], tp).wait_recv()
            total = total + got_in[src]
        full_in[tp] = total
        for step in range(1, tp_count):
            full_copy(step).start()

    @pl.when(sec < sections // 2)
    def _():
        project_inputs()

    def pass_middle(m):
        for zstep in range(1, nz):
            await_m(m, src_at(zstep, 0))
            for ystep in range(1, ny):
                relay_m_copy(m, zstep, ystep).start()

    @pl.loop(0, micro + 2)
    def _(it):
        with_middle = jnp.logical_and(jnp.logical_and(it >= 1, it <= micro), has_lower)
        lag = is_top.astype(jnp.int32)
        m_low = it - 1 - lag
        with_lower = jnp.logical_and(jnp.logical_and(m_low >= 0, m_low < micro), has_lower)

        @pl.when(jnp.logical_and(it < micro, jnp.logical_not(is_top)))
        def _():
            for zstep in range(nz):
                await_u(it, src_at(zstep, 0))
                for ystep in range(1, ny):
                    relay_u_copy(it, zstep, ystep).start()

        @pl.when(jnp.logical_and(with_middle, jnp.logical_not(is_top)))
        def _():
            pass_middle(it - 1)

        @pl.when(it == 0)
        def _():
            w_copy(1).wait()

        @pl.when(it == 1)
        def _():
            w_copy(0).wait()

        @pl.when(it < micro)
        def _():
            @pl.when(is_top)
            def _():
                for k in range(tp_count):
                    top_copy(it, k).wait()

            @pl.when(jnp.logical_and(is_top, it >= AHEAD))
            def _():
                pl.semaphore_wait(credit, 1)

            upper(it)

            @pl.when(sec == sections - 2)
            def _():
                pl.semaphore_signal(
                    credit, inc=1, device_id=(sec + 1, tp), device_id_type=MESH)

        @pl.when(jnp.logical_and(with_middle, is_top))
        def _():
            pass_middle(it - 1)

        @pl.when(with_lower)
        def _():
            lower(m_low)

    @pl.when(sec >= sections // 2)
    def _():
        project_inputs()

    for step in range(1, tp_count):
        src = lax.rem(tp + step, tp_count)
        tp_copy(full_in.at[src], full_in.at[src], send_my, full_recv.at[src], tp).wait_recv()
    lanes = 2 * rank_in
    pairs = EXAMPLES * rank_out
    product_all = lax.dot_general(
        out_v[...], full_in[...].reshape(micro * rows, lanes), (((0,), (0,)), ((), ())),
        precision=lax.Precision.HIGHEST, preferred_element_type=jnp.float32)
    lane = lax.broadcasted_iota(jnp.int32, (pairs, lanes), 1)
    grad_v[tp] = jnp.where(lane < rank_in, product_all[:pairs], product_all[pairs:])
    for step in range(1, tp_count):
        grad_copy(step).start()
    for step in range(1, tp_count):
        src = lax.rem(tp + step, tp_count)
        tp_copy(grad_v.at[src], grad_v.at[src], send_my, grad_recv.at[src], tp).wait_recv()
    total = grad_v[0]
    for k in range(1, tp_count):
        total = total + grad_v[k]
    sum_v[...] = total
    half = rank_out // 2
    number = q_ref.shape[1]
    sums = []
    for example in range(EXAMPLES):
        even = sum_v[pl.ds(example * rank_out, half, stride=2), :]
        odd = sum_v[pl.ds(example * rank_out + 1, half, stride=2), :]
        acc = jnp.zeros((number, lanes), jnp.float32)
        for layer in range(2):
            part = slice(layer * rank_in, (layer + 1) * rank_in)
            tiles = jnp.concatenate([even[:, part], odd[:, part]], 1)
            for j in range(half):
                block = q_ref[layer, :, j * lanes:(j + 1) * lanes].astype(jnp.float32)
                acc = acc + tiles[j:j + 1, :] * block
        sums.append(acc)
    score_v[sec] = lax.dot_general(
        jnp.ones((8, lanes), jnp.float32), jnp.concatenate(sums, 0), NT,
        precision=lax.Precision.HIGHEST, preferred_element_type=jnp.float32)
    for step in range(1, sections):
        score_copy(step).start()
    for step in range(1, sections):
        src = lax.rem(sec + step, sections)
        remote(score_v.at[src], score_v.at[src], send_my, score_recv.at[src], sec, tp).wait_recv()
    total = score_v[0]
    for k in range(1, sections):
        total = total + score_v[k]
    for example in range(EXAMPLES):
        score_ref[example:example + 1, :] = total[0:1, example * number:(example + 1) * number]

    @pl.when(is_top)
    def _():
        pl.semaphore_wait(credit, min(AHEAD, micro))

    for step in range(1, tp_count):
        part_copy(step).wait_send()
        full_copy(step).wait_send()
        grad_copy(step).wait_send()
    for step in range(1, sections):
        score_copy(step).wait_send()

    @pl.loop(0, micro)
    def _(m):
        @pl.when(jnp.logical_not(is_top))
        def _():
            for zstep in range(nz):
                for ystep in range(1, ny):
                    relay_u_copy(m, zstep, ystep).wait_send()

        @pl.when(has_lower)
        def _():
            for zstep in range(1, nz):
                middle_copy(m, zstep).wait_send()
            for zstep in range(nz):
                for ystep in range(1, ny):
                    relay_m_copy(m, zstep, ystep).wait_send()
                lower_copy(m, zstep).wait_send()


def shards(
    layer_inputs, weights, input_basis, output_basis, queries, top_cotangent, sequence_example
):
    sections = lax.axis_size("section")
    tp_count = lax.axis_size("tp")
    tokens, width = layer_inputs.shape[1:]
    micro = tp_count
    rows = tokens // micro
    nz, ny = grid_of(tp_count)
    lanes = 2 * input_basis.shape[2]
    pairs = EXAMPLES * output_basis.shape[2]
    number = queries.shape[1]
    dma = pltpu.SemaphoreType.DMA
    vmem = pl.BlockSpec(memory_space=pltpu.VMEM)
    hbm = pl.BlockSpec(memory_space=pl.ANY)
    smem = pl.BlockSpec(memory_space=pltpu.SMEM)
    return pl.pallas_call(
        functools.partial(chain_kernel, sections, tp_count),
        out_shape=jax.ShapeDtypeStruct((EXAMPLES, number), jnp.float32),
        in_specs=[hbm, hbm, vmem, vmem, vmem, vmem, smem],
        out_specs=vmem,
        scratch_shapes=[
            pltpu.VMEM((micro, tp_count, rows, width), jnp.bfloat16),
            pltpu.VMEM((micro, tp_count, rows, width), jnp.bfloat16),
            pltpu.VMEM((micro, rows, width), jnp.bfloat16),
            pltpu.VMEM(weights.shape, jnp.bfloat16),
            pltpu.VMEM((2, 2 * pairs, width), jnp.bfloat16),
            pltpu.VMEM((2, lanes, width), jnp.bfloat16),
            pltpu.VMEM((tokens, 2 * pairs), jnp.float32),
            pltpu.VMEM((tp_count, tokens // tp_count, lanes), jnp.float32),
            pltpu.VMEM((tp_count, tokens // tp_count, lanes), jnp.float32),
            pltpu.VMEM((tp_count, tokens // tp_count, lanes), jnp.float32),
            pltpu.VMEM((tp_count, pairs, lanes), jnp.float32),
            pltpu.VMEM((pairs, lanes), jnp.float32),
            pltpu.VMEM((sections, 8, EXAMPLES * number), jnp.float32),
            dma((2,)),
            dma((micro, tp_count)),
            dma((micro, tp_count)),
            dma((micro, nz)),
            dma,
            dma((micro, nz, ny)),
            dma((micro, nz, ny)),
            dma((micro, nz)),
            dma((tp_count,)),
            dma((tp_count,)),
            dma((tp_count,)),
            dma((tp_count,)),
            dma((tp_count,)),
            dma((tp_count,)),
            dma((sections,)),
            dma((sections,)),
            pltpu.SemaphoreType.REGULAR,
        ],
        compiler_params=pltpu.CompilerParams(
            collective_id=0, has_side_effects=True, vmem_limit_bytes=56 * 2**20),
    )(
        top_cotangent, weights, layer_inputs, jnp.swapaxes(input_basis, 1, 2),
        jnp.swapaxes(output_basis, 1, 2), queries, sequence_example)


def solution(mesh):
    placed = (
        P("section", None, "tp"),
        P("section", "tp", None),
        P("section", "tp", None),
        P("section", "tp", None),
        P("section", "tp", None),
        P(),
        P(),
    )
    return jax.shard_map(
        shards, mesh=mesh, in_specs=placed, out_specs=P(None, "tp"), check_vma=False
    )
```

profile of v0, /device:TPU:0, one launch (start us, length us, event | category | flops | bytes accessed | tf_op | source)
XLA Modules:
  0.0 165.0 jit_solution(2149510607902695910)
XLA Ops:
  0.0 163.8 %shard_map.73 = f32[2,64]{1,0:T(2,128)} custom-call(bf16[512,4096]{1,0:T(8,128)(2,1)} %top_ref.1, bf16[2,512,4096]{2,1,0:T(8,128)(2,1)} %w_ref.1, bf16[2,512,512]{2,1,0:T(8,128)(2,1)} %h_ref.1, bf16[2,64,512]{2,1,0:T(8,128)(2,1)} %bitcast.2, bf16[2,32,512]{2,1,0:T(8,128)(2,1)} %bitcast.3, bf16[2,64,2048]{2,1,0:T(8,128)(2,1)} %q_ref.1, s32[4]{0:T(128)} %se_ref.1), custom_call_target="tpu_custom_call" | custom-call | tf_op jit(solution)/shard_map/pallas_call | solution.py:406
  163.8 1.2 copy.9
where the time goes:
time: 165 us
  Pallas kernels  164 us (99%)
    pallas_call x1, Pallas kernels, shards(): pl.pallas_call(functools.partial(chain_kernel, sections, tp_count), out_s...  164 us

commit v1 on v0

--- a/solution.py
+++ b/solution.py
@@ -8,7 +8,7 @@
 from jax.sharding import PartitionSpec as P
 
 EXAMPLES = 2
-AHEAD = 4
+ROWS = 32
 MESH = pl.DeviceIdType.MESH
 NT = (((1,), (1,)), ((), ()))
 
@@ -29,8 +29,8 @@
 def chain_kernel(
     sections, tp_count, top_ref, w_ref, h_ref, ib_ref, ob_ref, q_ref, se_ref, score_ref,
     buf_u, buf_m, buf_l, w_v, ob_v, ib_v, out_v, part_in, got_in, full_in, grad_v, sum_v, score_v,
-    w_sem, recv_u, recv_m, send_m, send_my, relay_u, relay_m, send_l,
-    part_send, part_recv, full_send, full_recv, grad_send, grad_recv, score_send, score_recv, credit,
+    w_sem, recv_u, recv_m, send_m, send_u, send_my, relay_u, relay_m, send_l, send_ly,
+    part_send, part_recv, full_send, full_recv, grad_send, grad_recv, score_send, score_recv,
 ):
     nz, ny = grid_of(tp_count)
     sec = lax.axis_index("section")
@@ -39,6 +39,9 @@
     micro, _, rows, width = buf_u.shape
     is_top = sec == sections - 1
     has_lower = sec > 0
+    pair_lower = lax.rem(sec, 2) == 1
+    pair_upper = jnp.logical_not(pair_lower)
+    far_fed = jnp.logical_and(pair_lower, jnp.logical_not(is_top))
 
     far = [z]
     for k in range(nz - 1):
@@ -91,7 +94,10 @@
                 top_copy(m, k).start()
 
     w_copy(1).start()
-    w_copy(0).start()
+
+    @pl.when(has_lower)
+    def _():
+        w_copy(0).start()
 
     barrier = pltpu.get_barrier_semaphore()
 
@@ -101,26 +107,16 @@
     for step in range(1, tp_count):
         greet(sec, lax.rem(tp + step, tp_count))
 
-    @pl.when(has_lower)
-    def _():
-        for step in range(nz):
-            greet(sec - 1, peer_z(step))
-
-    @pl.when(jnp.logical_not(is_top))
-    def _():
-        for step in range(nz):
-            greet(sec + 1, peer_z(step))
-
+    partner = sec + 1 - 2 * lax.rem(sec, 2)
+    for step in range(1, nz):
+        greet(partner, peer_z(step))
+    for step in range(1, ny):
+        greet(partner, peer_y(step))
     for step in range(1, sections):
-        other = lax.rem(sec + step, sections)
-
-        @pl.when(jnp.logical_and(other != sec + 1, other != sec - 1))
-        def _(other=other):
-            greet(other, tp)
+        greet(lax.rem(sec + step, sections), tp)
 
     prepare_bases()
-    linked = has_lower.astype(jnp.int32) + jnp.logical_not(is_top).astype(jnp.int32)
-    pl.semaphore_wait(barrier, tp_count + sections - 2 + (nz - 1) * linked)
+    pl.semaphore_wait(barrier, tp_count + nz + ny + sections - 4)
 
     def relay_u_copy(m, zstep, ystep):
         src = src_at(zstep, 0)
@@ -136,9 +132,17 @@
         return remote(buf_m.at[m, tp], buf_m.at[m, tp], send_m.at[m, zstep],
                       recv_m.at[m, tp], sec, peer_z(zstep))
 
+    def upper_copy(m, zstep):
+        return remote(buf_u.at[m, tp], buf_u.at[m, tp], send_u.at[m, zstep],
+                      recv_u.at[m, tp], sec, peer_z(zstep))
+
     def lower_copy(m, zstep):
         return remote(buf_l.at[m], buf_u.at[m, tp], send_l.at[m, zstep],
                       recv_u.at[m, tp], sec - 1, peer_z(zstep))
+
+    def lower_y_copy(m, ystep):
+        return remote(buf_l.at[m], buf_u.at[m, tp], send_ly.at[m, ystep],
+                      recv_u.at[m, tp], sec - 1, peer_y(ystep))
 
     def await_u(m, src):
         remote(buf_u.at[m, src], buf_u.at[m, src], send_my, recv_u.at[m, src], sec, tp).wait_recv()
@@ -196,8 +200,15 @@
                 await_m(m, src_at(zstep, ystep))
             total = product(buf_m, m, 0, ystep, total)
         buf_l[m] = (floats + slope * total).astype(jnp.bfloat16)
-        for step in [*range(1, nz), 0]:
-            lower_copy(m, step).start()
+
+        @pl.when(pair_lower)
+        def _():
+            for step in range(1, nz):
+                lower_copy(m, step).start()
+            for step in range(1, ny):
+                lower_y_copy(m, step).start()
+
+        lower_copy(m, 0).start()
 
     def tp_copy(src, dst, ssem, rsem, to_tp):
         return remote(src, dst, ssem, rsem, sec, to_tp)
@@ -249,61 +260,72 @@
     def _():
         project_inputs()
 
+    def spread_upper(m):
+        await_u(m, tp)
+        for step in range(1, nz):
+            upper_copy(m, step).start()
+        for step in range(1, ny):
+            relay_u_copy(m, 0, step).start()
+
+    def pass_upper(m):
+        @pl.when(pair_upper)
+        def _():
+            await_u(m, tp)
+
+        for zstep in range(1, nz):
+            await_u(m, src_at(zstep, 0))
+            for ystep in range(1, ny):
+                relay_u_copy(m, zstep, ystep).start()
+
     def pass_middle(m):
         for zstep in range(1, nz):
             await_m(m, src_at(zstep, 0))
             for ystep in range(1, ny):
                 relay_m_copy(m, zstep, ystep).start()
 
-    @pl.loop(0, micro + 2)
+    def within(m):
+        return jnp.logical_and(m >= 0, m < micro)
+
+    lag_pass = far_fed.astype(jnp.int32)
+    lag_upper = jnp.where(is_top, 0, lag_pass + 1)
+
+    @pl.loop(0, micro + 5)
     def _(it):
-        with_middle = jnp.logical_and(jnp.logical_and(it >= 1, it <= micro), has_lower)
-        lag = is_top.astype(jnp.int32)
-        m_low = it - 1 - lag
-        with_lower = jnp.logical_and(jnp.logical_and(m_low >= 0, m_low < micro), has_lower)
-
-        @pl.when(jnp.logical_and(it < micro, jnp.logical_not(is_top)))
-        def _():
-            for zstep in range(nz):
-                await_u(it, src_at(zstep, 0))
-                for ystep in range(1, ny):
-                    relay_u_copy(it, zstep, ystep).start()
-
-        @pl.when(jnp.logical_and(with_middle, jnp.logical_not(is_top)))
-        def _():
-            pass_middle(it - 1)
-
-        @pl.when(it == 0)
+        m_pass = it - lag_pass
+        m_up = it - lag_upper
+        m_mid = m_up - 1
+        m_low = m_up - 2
+
+        @pl.when(jnp.logical_and(it < micro, far_fed))
+        def _():
+            spread_upper(it)
+
+        @pl.when(jnp.logical_and(within(m_pass), jnp.logical_not(is_top)))
+        def _():
+            pass_upper(m_pass)
+
+        @pl.when(m_up == 0)
         def _():
             w_copy(1).wait()
 
-        @pl.when(it == 1)
-        def _():
-            w_copy(0).wait()
-
-        @pl.when(it < micro)
+        @pl.when(within(m_up))
         def _():
             @pl.when(is_top)
             def _():
                 for k in range(tp_count):
-                    top_copy(it, k).wait()
-
-            @pl.when(jnp.logical_and(is_top, it >= AHEAD))
-            def _():
-                pl.semaphore_wait(credit, 1)
-
-            upper(it)
-
-            @pl.when(sec == sections - 2)
-            def _():
-                pl.semaphore_signal(
-                    credit, inc=1, device_id=(sec + 1, tp), device_id_type=MESH)
-
-        @pl.when(jnp.logical_and(with_middle, is_top))
-        def _():
-            pass_middle(it - 1)
-
-        @pl.when(with_lower)
+                    top_copy(m_up, k).wait()
+
+            upper(m_up)
+
+        @pl.when(jnp.logical_and(within(m_mid), has_lower))
+        def _():
+            pass_middle(m_mid)
+
+        @pl.when(jnp.logical_and(m_low == 0, has_lower))
+        def _():
+            w_copy(0).wait()
+
+        @pl.when(jnp.logical_and(within(m_low), has_lower))
         def _():
             lower(m_low)
 
@@ -358,10 +380,6 @@
     for example in range(EXAMPLES):
         score_ref[example:example + 1, :] = total[0:1, example * number:(example + 1) * number]
 
-    @pl.when(is_top)
-    def _():
-        pl.semaphore_wait(credit, min(AHEAD, micro))
-
     for step in range(1, tp_count):
         part_copy(step).wait_send()
         full_copy(step).wait_send()
@@ -371,9 +389,16 @@
 
     @pl.loop(0, micro)
     def _(m):
+        @pl.when(far_fed)
+        def _():
+            for zstep in range(1, nz):
+                upper_copy(m, zstep).wait_send()
+            for ystep in range(1, ny):
+                relay_u_copy(m, 0, ystep).wait_send()
+
         @pl.when(jnp.logical_not(is_top))
         def _():
-            for zstep in range(nz):
+            for zstep in range(1, nz):
                 for ystep in range(1, ny):
                     relay_u_copy(m, zstep, ystep).wait_send()
 
@@ -384,7 +409,14 @@
             for zstep in range(nz):
                 for ystep in range(1, ny):
                     relay_m_copy(m, zstep, ystep).wait_send()
+            lower_copy(m, 0).wait_send()
+
+        @pl.when(pair_lower)
+        def _():
+            for zstep in range(1, nz):
                 lower_copy(m, zstep).wait_send()
+            for ystep in range(1, ny):
+                lower_y_copy(m, ystep).wait_send()
 
 
 def shards(
@@ -393,8 +425,8 @@
     sections = lax.axis_size("section")
     tp_count = lax.axis_size("tp")
     tokens, width = layer_inputs.shape[1:]
-    micro = tp_count
-    rows = tokens // micro
+    rows = ROWS
+    micro = tokens // rows
     nz, ny = grid_of(tp_count)
     lanes = 2 * input_basis.shape[2]
     pairs = EXAMPLES * output_basis.shape[2]
@@ -426,10 +458,12 @@
             dma((micro, tp_count)),
             dma((micro, tp_count)),
             dma((micro, nz)),
+            dma((micro, nz)),
             dma,
             dma((micro, nz, ny)),
             dma((micro, nz, ny)),
             dma((micro, nz)),
+            dma((micro, ny)),
             dma((tp_count,)),
             dma((tp_count,)),
             dma((tp_count,)),
@@ -438,7 +472,6 @@
             dma((tp_count,)),
             dma((sections,)),
             dma((sections,)),
-            pltpu.SemaphoreType.REGULAR,
         ],
         compiler_params=pltpu.CompilerParams(
             collective_id=0, has_side_effects=True, vmem_limit_bytes=56 * 2**20),

time: 165 us -> 146 us (0.88)
  Pallas kernels: 164 us -> 145 us
    pallas_call x1, Pallas kernels: 164 us -> 145 us  [shards(): pl.pallas_call(functools.partial(chain_kernel, sections, tp_count), out_s...]
where the time goes in v1:
time: 146 us
  Pallas kernels  145 us (99%)
    pallas_call x1, Pallas kernels, shards(): pl.pallas_call(functools.partial(chain_kernel, sections, tp_count), out_s...  145 us

profile of v1, /device:TPU:0, one launch (start us, length us, event | category | flops | bytes accessed | tf_op | source)
XLA Modules:
  0.0 146.0 jit_solution(8987305731238161948)
XLA Ops:
  0.0 144.7 %shard_map.73 = f32[2,64]{1,0:T(2,128)} custom-call(bf16[512,4096]{1,0:T(8,128)(2,1)} %top_ref.1, bf16[2,512,4096]{2,1,0:T(8,128)(2,1)} %w_ref.1, bf16[2,512,512]{2,1,0:T(8,128)(2,1)} %h_ref.1, bf16[2,64,512]{2,1,0:T(8,128)(2,1)} %bitcast.2, bf16[2,32,512]{2,1,0:T(8,128)(2,1)} %bitcast.3, bf16[2,64,2048]{2,1,0:T(8,128)(2,1)} %q_ref.1, s32[4]{0:T(128)} %se_ref.1), custom_call_target="tpu_custom_call" | custom-call | tf_op jit(solution)/shard_map/pallas_call | solution.py:438
  144.7 1.2 copy.9

commit v2 on v1

--- a/solution.py
+++ b/solution.py
@@ -9,8 +9,12 @@
 
 EXAMPLES = 2
 ROWS = 32
+TOP_ROUTED = (0, 0)
+LOW_ROUTED = (0, 0)
+LAGS = ((0, 0, 1, 2), (0, 1, 2, 3), (1, 2, 3, 4), (0, 1, 1, 1))
 MESH = pl.DeviceIdType.MESH
 NT = (((1,), (1,)), ((), ()))
+NN = (((1,), (0,)), ((), ()))
 
 
 def grid_of(tp_count):
@@ -28,8 +32,8 @@
 
 def chain_kernel(
     sections, tp_count, top_ref, w_ref, h_ref, ib_ref, ob_ref, q_ref, se_ref, score_ref,
-    buf_u, buf_m, buf_l, w_v, ob_v, ib_v, out_v, part_in, got_in, full_in, grad_v, sum_v, score_v,
-    w_sem, recv_u, recv_m, send_m, send_u, send_my, relay_u, relay_m, send_l, send_ly,
+    buf_u, buf_m, buf_l, buf_v, w_v, w_t, ob_v, ib_v, out_v, part_in, got_in, full_in, grad_v, sum_v, score_v,
+    w_sem, top_sem, recv_x, recv_u, recv_m, near_u, near_m, recv_v, send_u, send_m, send_l, send_v, send_my,
     part_send, part_recv, full_send, full_recv, grad_send, grad_recv, score_send, score_recv,
 ):
     nz, ny = grid_of(tp_count)
@@ -41,6 +45,17 @@
     has_lower = sec > 0
     pair_lower = lax.rem(sec, 2) == 1
     pair_upper = jnp.logical_not(pair_lower)
+    relays = sorted({(sections - 1, sections - 4), (3, 0)}) if sections >= 4 else []
+
+    def in_span(m, span):
+        return jnp.logical_and(m >= span[0], m < span[1])
+
+    def top_routed(m):
+        return in_span(m, TOP_ROUTED if relays else (0, 0))
+
+    def low_routed(m):
+        return in_span(m, LOW_ROUTED if relays else (0, 0))
+
     far_fed = jnp.logical_and(pair_lower, jnp.logical_not(is_top))
 
     far = [z]
@@ -50,6 +65,7 @@
         from_high = k + (z <= k).astype(jnp.int32)
         far.append(jnp.where(z < nz // 2, from_low, from_high))
     near = far[:1] + far[:0:-1]
+    mate = z + 1 - 2 * lax.rem(z, 2)
 
     def peer_z(step):
         return far[step] * ny + y
@@ -66,7 +82,7 @@
     def top_copy(m, k):
         return pltpu.make_async_copy(
             top_ref.at[pl.ds(pl.multiple_of(m * rows, rows), rows), pl.ds(k * width, width)],
-            buf_u.at[m, k], recv_u.at[m, k])
+            buf_u.at[m, k], top_sem.at[m])
 
     def remote(src, dst, ssem, rsem, to_sec, to_tp):
         return pltpu.make_async_remote_copy(
@@ -114,48 +130,94 @@
         greet(partner, peer_y(step))
     for step in range(1, sections):
         greet(lax.rem(sec + step, sections), tp)
+    linked = 0
+    for pair in relays:
+        for here, there in (pair, pair[::-1]):
+            @pl.when(sec == here)
+            def _(there=there):
+                for step in range(1, tp_count):
+                    greet(there, lax.rem(tp + step, tp_count))
+
+            linked = linked + (sec == here).astype(jnp.int32)
+
+    def turn_weights(layer):
+        w_copy(layer).wait()
+
+        @pl.loop(0, tp_count)
+        def _(k):
+            columns = pl.ds(pl.multiple_of(k * width, width), width)
+            w_t[layer, columns, :] = w_v[layer, :, columns].T
 
     prepare_bases()
-    pl.semaphore_wait(barrier, tp_count + nz + ny + sections - 4)
-
-    def relay_u_copy(m, zstep, ystep):
+    turn_weights(1)
+
+    @pl.when(jnp.logical_and(has_lower, jnp.logical_not(is_top)))
+    def _():
+        turn_weights(0)
+
+    pl.semaphore_wait(barrier, tp_count + nz + ny + sections - 4 + (tp_count - 1) * linked)
+
+    def slots(buf, m, count, ssem, rsem):
+        part = buf.at[m, pl.ds(0, count)]
+        return remote(part, part, ssem, rsem, sec, tp)
+
+    def relay_copy(buf, sends, recvs, m, zstep, ystep):
         src = src_at(zstep, 0)
-        return remote(buf_u.at[m, src], buf_u.at[m, src], relay_u.at[m, zstep, ystep],
-                      recv_u.at[m, src], sec, peer_y(ystep))
-
-    def relay_m_copy(m, zstep, ystep):
-        src = src_at(zstep, 0)
-        return remote(buf_m.at[m, src], buf_m.at[m, src], relay_m.at[m, zstep, ystep],
-                      recv_m.at[m, src], sec, peer_y(ystep))
-
-    def middle_copy(m, zstep):
-        return remote(buf_m.at[m, tp], buf_m.at[m, tp], send_m.at[m, zstep],
-                      recv_m.at[m, tp], sec, peer_z(zstep))
-
-    def upper_copy(m, zstep):
-        return remote(buf_u.at[m, tp], buf_u.at[m, tp], send_u.at[m, zstep],
-                      recv_u.at[m, tp], sec, peer_z(zstep))
-
-    def lower_copy(m, zstep):
-        return remote(buf_l.at[m], buf_u.at[m, tp], send_l.at[m, zstep],
-                      recv_u.at[m, tp], sec - 1, peer_z(zstep))
+        return remote(buf.at[m, src], buf.at[m, src], sends.at[m],
+                      recvs.at[m, ny - ystep], sec, peer_y(ystep))
+
+    def forward_copy(buf, sends, recvs, m, ystep):
+        src = src_at(0, ystep)
+        return remote(buf.at[m, src], buf.at[m, src], sends.at[m],
+                      recvs.at[m, ystep], sec, mate * ny + y)
+
+    def spread_copy(buf, sends, recvs, m, zstep):
+        return remote(buf.at[m, tp], buf.at[m, tp], sends.at[m], recvs.at[m, 0], sec, peer_z(zstep))
+
+    def lower_own_copy(m):
+        return remote(buf_l.at[m], buf_u.at[m, tp], send_l.at[m], recv_x.at[m], sec - 1, tp)
+
+    def lower_z_copy(m, zstep):
+        return remote(buf_l.at[m], buf_u.at[m, tp], send_l.at[m], recv_u.at[m, 0],
+                      sec - 1, peer_z(zstep))
 
     def lower_y_copy(m, ystep):
-        return remote(buf_l.at[m], buf_u.at[m, tp], send_ly.at[m, ystep],
-                      recv_u.at[m, tp], sec - 1, peer_y(ystep))
-
-    def await_u(m, src):
-        remote(buf_u.at[m, src], buf_u.at[m, src], send_my, recv_u.at[m, src], sec, tp).wait_recv()
-
-    def await_m(m, src):
-        remote(buf_m.at[m, src], buf_m.at[m, src], send_my, recv_m.at[m, src], sec, tp).wait_recv()
+        return remote(buf_l.at[m], buf_u.at[m, tp], send_l.at[m], near_u.at[m, ny - ystep],
+                      sec - 1, peer_y(ystep))
+
+    def await_own(m):
+        remote(buf_u.at[m, tp], buf_u.at[m, tp], send_my, recv_x.at[m], sec, tp).wait_recv()
+
+    def await_line(buf, recvs, m, ystep):
+        slots(buf, m, nz - 1, send_my, recvs.at[m, ystep]).wait_recv()
+
+    def await_near(buf, nears, m, ystep):
+        slots(buf, m, 1, send_my, nears.at[m, ystep]).wait_recv()
+
+    def pass_on(buf, sends, recvs, nears, m):
+        for ystep in range(1, ny):
+            await_near(buf, nears, m, ystep)
+            forward_copy(buf, sends, recvs, m, ystep).start()
+        await_line(buf, recvs, m, 0)
+        for zstep in range(2, nz):
+            for ystep in range(1, ny):
+                relay_copy(buf, sends, recvs, m, zstep, ystep).start()
+
+    def routed_on(buf, recvs, nears, m, target):
+        remote(buf_v.at[m], buf_v.at[m], send_my, recv_v.at[m], sec, tp).wait_recv()
+        for zstep in [*range(nz - 1, 0, -1), 0]:
+            for ystep in range(ny):
+                if zstep or ystep:
+                    sem = recvs if zstep else nears
+                    remote(buf_v.at[m], buf.at[m, tp], send_v.at[m], sem.at[m, (ny - ystep) % ny],
+                           target, src_at(zstep, ystep)).start()
 
     def product(buf, m, layer, ystep, total=None):
         for zstep in range(nz):
             src = src_at(zstep, ystep)
             columns = pl.ds(pl.multiple_of(src * width, width), width)
             term = lax.dot_general(
-                buf[m, src], w_v[layer, :, columns], NT, preferred_element_type=jnp.float32)
+                buf[m, src], w_t[layer, columns, :], NN, preferred_element_type=jnp.float32)
             total = term if total is None else total + term
         return total
 
@@ -164,23 +226,37 @@
         own = buf_u[m, tp]
         floats = own.astype(jnp.float32)
         slope = slope_of(h_ref[1, at, :])
+
+        @pl.when(jnp.logical_and(sec == 0, low_routed(m)))
+        def _():
+            await_line(buf_u, recv_u, m, 0)
+            for ystep in range(1, ny):
+                await_near(buf_u, near_u, m, ystep)
+
         total = product(buf_u, m, 1, 0)
         for ystep in range(1, ny):
             @pl.when(jnp.logical_not(is_top))
             def _(ystep=ystep):
-                for zstep in range(nz):
-                    await_u(m, src_at(zstep, ystep))
+                await_line(buf_u, recv_u, m, ystep)
 
             total = product(buf_u, m, 1, ystep, total)
         middle = (floats + slope * total).astype(jnp.bfloat16)
         buf_m[m, tp] = middle
 
-        @pl.when(has_lower)
+        routed = jnp.logical_and(is_top, top_routed(m))
+
+        @pl.when(jnp.logical_and(has_lower, jnp.logical_not(routed)))
         def _():
             for step in range(1, nz):
-                middle_copy(m, step).start()
+                spread_copy(buf_m, send_m, recv_m, m, step).start()
             for step in range(1, ny):
-                relay_m_copy(m, 0, step).start()
+                relay_copy(buf_m, send_m, near_m, m, 0, step).start()
+
+        if relays:
+            @pl.when(routed)
+            def _():
+                remote(buf_m.at[m, tp], buf_v.at[m], send_m.at[m], recv_v.at[m],
+                       sections - 4, tp).start()
 
         feats = lax.dot_general(
             own, ob_v[1], NT, preferred_element_type=jnp.float32
@@ -194,21 +270,34 @@
         at = pl.ds(pl.multiple_of(m * rows, rows), rows)
         floats = buf_m[m, tp].astype(jnp.float32)
         slope = slope_of(h_ref[0, at, :])
+
+        @pl.when(jnp.logical_and(is_top, top_routed(m)))
+        def _():
+            await_line(buf_m, recv_m, m, 0)
+            for ystep in range(1, ny):
+                await_near(buf_m, near_m, m, ystep)
+
         total = product(buf_m, m, 0, 0)
         for ystep in range(1, ny):
-            for zstep in range(nz):
-                await_m(m, src_at(zstep, ystep))
+            await_line(buf_m, recv_m, m, ystep)
             total = product(buf_m, m, 0, ystep, total)
         buf_l[m] = (floats + slope * total).astype(jnp.bfloat16)
 
-        @pl.when(pair_lower)
+        routed = jnp.logical_and(sec == 1, low_routed(m))
+
+        @pl.when(jnp.logical_and(pair_lower, jnp.logical_not(routed)))
         def _():
             for step in range(1, nz):
-                lower_copy(m, step).start()
+                lower_z_copy(m, step).start()
             for step in range(1, ny):
                 lower_y_copy(m, step).start()
 
-        lower_copy(m, 0).start()
+        if relays:
+            @pl.when(routed)
+            def _():
+                remote(buf_l.at[m], buf_v.at[m], send_l.at[m], recv_v.at[m], 3, tp).start()
+
+        lower_own_copy(m).start()
 
     def tp_copy(src, dst, ssem, rsem, to_tp):
         return remote(src, dst, ssem, rsem, sec, to_tp)
@@ -261,40 +350,53 @@
         project_inputs()
 
     def spread_upper(m):
-        await_u(m, tp)
+        await_own(m)
         for step in range(1, nz):
-            upper_copy(m, step).start()
+            spread_copy(buf_u, send_u, recv_u, m, step).start()
         for step in range(1, ny):
-            relay_u_copy(m, 0, step).start()
+            relay_copy(buf_u, send_u, near_u, m, 0, step).start()
 
     def pass_upper(m):
         @pl.when(pair_upper)
         def _():
-            await_u(m, tp)
-
-        for zstep in range(1, nz):
-            await_u(m, src_at(zstep, 0))
-            for ystep in range(1, ny):
-                relay_u_copy(m, zstep, ystep).start()
+            await_own(m)
+
+        @pl.when(jnp.logical_not(jnp.logical_and(sec == 0, low_routed(m))))
+        def _():
+            pass_on(buf_u, send_u, recv_u, near_u, m)
 
     def pass_middle(m):
-        for zstep in range(1, nz):
-            await_m(m, src_at(zstep, 0))
-            for ystep in range(1, ny):
-                relay_m_copy(m, zstep, ystep).start()
+        @pl.when(jnp.logical_not(jnp.logical_and(is_top, top_routed(m))))
+        def _():
+            pass_on(buf_m, send_m, recv_m, near_m, m)
 
     def within(m):
         return jnp.logical_and(m >= 0, m < micro)
 
-    lag_pass = far_fed.astype(jnp.int32)
-    lag_upper = jnp.where(is_top, 0, lag_pass + 1)
-
-    @pl.loop(0, micro + 5)
+    kind = jnp.where(is_top, 0, jnp.where(far_fed, 2, jnp.where(has_lower, 1, 3)))
+
+    def lag_of(k):
+        lag = LAGS[0][k]
+        for other in range(1, 4):
+            lag = jnp.where(kind == other, LAGS[other][k], lag)
+        return lag
+
+    lag_pass, lag_upper, lag_middle, lag_lower = [lag_of(k) for k in range(4)]
+    steps = micro + max(max(lags) for lags in LAGS)
+
+    if relays:
+        @pl.when(sec == sections - 4)
+        def _():
+            @pl.loop(*TOP_ROUTED)
+            def _(m):
+                routed_on(buf_m, recv_m, near_m, m, sections - 1)
+
+    @pl.loop(0, steps)
     def _(it):
         m_pass = it - lag_pass
         m_up = it - lag_upper
-        m_mid = m_up - 1
-        m_low = m_up - 2
+        m_mid = it - lag_middle
+        m_low = it - lag_lower
 
         @pl.when(jnp.logical_and(it < micro, far_fed))
         def _():
@@ -303,27 +405,23 @@
         @pl.when(jnp.logical_and(within(m_pass), jnp.logical_not(is_top)))
         def _():
             pass_upper(m_pass)
-
-        @pl.when(m_up == 0)
-        def _():
-            w_copy(1).wait()
 
         @pl.when(within(m_up))
         def _():
             @pl.when(is_top)
             def _():
-                for k in range(tp_count):
-                    top_copy(m_up, k).wait()
+                pltpu.make_async_copy(
+                    buf_u.at[m_up], buf_u.at[m_up], top_sem.at[m_up]).wait()
 
             upper(m_up)
 
+        @pl.when(jnp.logical_and(it == 0, is_top))
+        def _():
+            turn_weights(0)
+
         @pl.when(jnp.logical_and(within(m_mid), has_lower))
         def _():
             pass_middle(m_mid)
-
-        @pl.when(jnp.logical_and(m_low == 0, has_lower))
-        def _():
-            w_copy(0).wait()
 
         @pl.when(jnp.logical_and(within(m_low), has_lower))
         def _():
@@ -332,6 +430,13 @@
     @pl.when(sec >= sections // 2)
     def _():
         project_inputs()
+
+    if relays:
+        @pl.when(sec == 3)
+        def _():
+            @pl.loop(*LOW_ROUTED)
+            def _(m):
+                routed_on(buf_u, recv_u, near_u, m, 0)
 
     for step in range(1, tp_count):
         src = lax.rem(tp + step, tp_count)
@@ -342,15 +447,16 @@
         out_v[...], full_in[...].reshape(micro * rows, lanes), (((0,), (0,)), ((), ())),
         precision=lax.Precision.HIGHEST, preferred_element_type=jnp.float32)
     lane = lax.broadcasted_iota(jnp.int32, (pairs, lanes), 1)
-    grad_v[tp] = jnp.where(lane < rank_in, product_all[:pairs], product_all[pairs:])
+    own_grad = jnp.where(lane < rank_in, product_all[:pairs], product_all[pairs:])
+    grad_v[tp] = own_grad.astype(jnp.bfloat16)
     for step in range(1, tp_count):
         grad_copy(step).start()
     for step in range(1, tp_count):
         src = lax.rem(tp + step, tp_count)
         tp_copy(grad_v.at[src], grad_v.at[src], send_my, grad_recv.at[src], tp).wait_recv()
-    total = grad_v[0]
+    total = grad_v[0].astype(jnp.float32)
     for k in range(1, tp_count):
-        total = total + grad_v[k]
+        total = total + grad_v[k].astype(jnp.float32)
     sum_v[...] = total
     half = rank_out // 2
     number = q_ref.shape[1]
@@ -387,36 +493,28 @@
     for step in range(1, sections):
         score_copy(step).wait_send()
 
+    def sent(sends, buf, m, count, when):
+        @pl.when(when)
+        def _():
+            slots(buf, m, count, sends.at[m], send_my).wait_send()
+
     @pl.loop(0, micro)
     def _(m):
-        @pl.when(far_fed)
-        def _():
-            for zstep in range(1, nz):
-                upper_copy(m, zstep).wait_send()
-            for ystep in range(1, ny):
-                relay_u_copy(m, 0, ystep).wait_send()
-
-        @pl.when(jnp.logical_not(is_top))
-        def _():
-            for zstep in range(1, nz):
-                for ystep in range(1, ny):
-                    relay_u_copy(m, zstep, ystep).wait_send()
-
-        @pl.when(has_lower)
-        def _():
-            for zstep in range(1, nz):
-                middle_copy(m, zstep).wait_send()
-            for zstep in range(nz):
-                for ystep in range(1, ny):
-                    relay_m_copy(m, zstep, ystep).wait_send()
-            lower_copy(m, 0).wait_send()
-
-        @pl.when(pair_lower)
-        def _():
-            for zstep in range(1, nz):
-                lower_copy(m, zstep).wait_send()
-            for ystep in range(1, ny):
-                lower_y_copy(m, ystep).wait_send()
+        top_far = jnp.logical_and(is_top, top_routed(m))
+        low_far = jnp.logical_and(sec == 1, low_routed(m))
+        in_far = jnp.logical_and(sec == 0, low_routed(m))
+        sent(send_u, buf_u, m, tp_count - 1, far_fed)
+        sent(send_u, buf_u, m, (nz - 1) * (ny - 1),
+             jnp.logical_and(jnp.logical_and(pair_upper, ny > 1), jnp.logical_not(in_far)))
+        sent(send_m, buf_m, m, tp_count - 1, jnp.logical_and(has_lower, jnp.logical_not(top_far)))
+        sent(send_m, buf_m, m, 1, top_far)
+        sent(send_l, buf_u, m, nz + ny - 1, jnp.logical_and(pair_lower, jnp.logical_not(low_far)))
+        sent(send_l, buf_u, m, 2, low_far)
+        sent(send_l, buf_u, m, 1, jnp.logical_and(pair_upper, has_lower))
+        if relays:
+            sent(send_v, buf_u, m, tp_count - 1, jnp.logical_or(
+                jnp.logical_and(sec == sections - 4, top_routed(m)),
+                jnp.logical_and(sec == 3, low_routed(m))))
 
 
 def shards(
@@ -444,26 +542,31 @@
             pltpu.VMEM((micro, tp_count, rows, width), jnp.bfloat16),
             pltpu.VMEM((micro, tp_count, rows, width), jnp.bfloat16),
             pltpu.VMEM((micro, rows, width), jnp.bfloat16),
+            pltpu.VMEM((micro, rows, width), jnp.bfloat16),
             pltpu.VMEM(weights.shape, jnp.bfloat16),
+            pltpu.VMEM((2, weights.shape[2], width), jnp.bfloat16),
             pltpu.VMEM((2, 2 * pairs, width), jnp.bfloat16),
             pltpu.VMEM((2, lanes, width), jnp.bfloat16),
             pltpu.VMEM((tokens, 2 * pairs), jnp.float32),
             pltpu.VMEM((tp_count, tokens // tp_count, lanes), jnp.float32),
             pltpu.VMEM((tp_count, tokens // tp_count, lanes), jnp.float32),
             pltpu.VMEM((tp_count, tokens // tp_count, lanes), jnp.float32),
-            pltpu.VMEM((tp_count, pairs, lanes), jnp.float32),
+            pltpu.VMEM((tp_count, pairs, lanes), jnp.bfloat16),
             pltpu.VMEM((pairs, lanes), jnp.float32),
             pltpu.VMEM((sections, 8, EXAMPLES * number), jnp.float32),
             dma((2,)),
-            dma((micro, tp_count)),
-            dma((micro, tp_count)),
-            dma((micro, nz)),
-            dma((micro, nz)),
+            dma((micro,)),
+            dma((micro,)),
+            dma((micro, ny)),
+            dma((micro, ny)),
+            dma((micro, ny)),
+            dma((micro, ny)),
+            dma((micro,)),
+            dma((micro,)),
+            dma((micro,)),
+            dma((micro,)),
+            dma((micro,)),
             dma,
-            dma((micro, nz, ny)),
-            dma((micro, nz, ny)),
-            dma((micro, nz)),
-            dma((micro, ny)),
             dma((tp_count,)),
             dma((tp_count,)),
             dma((tp_count,)),

time: 146 us -> 136 us (0.932)
  Pallas kernels: 145 us -> 134 us
    pallas_call x1, Pallas kernels: 145 us -> 134 us  [shards(): pl.pallas_call(functools.partial(chain_kernel, sections, tp_count), out_s...]
where the time goes in v2:
time: 136 us; the launch traced here: 135 us
  Pallas kernels  134 us (99%)
    pallas_call x1, Pallas kernels, shards(): pl.pallas_call(functools.partial(chain_kernel, sections, tp_count), out_s...  134 us

profile of v2, /device:TPU:0, one launch (start us, length us, event | category | flops | bytes accessed | tf_op | source)
XLA Modules:
  0.0 135.5 jit_solution(10259717856047846923)
XLA Ops:
  0.0 134.2 %shard_map.73 = f32[2,64]{1,0:T(2,128)} custom-call(bf16[512,4096]{1,0:T(8,128)(2,1)} %top_ref.1, bf16[2,512,4096]{2,1,0:T(8,128)(2,1)} %w_ref.1, bf16[2,512,512]{2,1,0:T(8,128)(2,1)} %h_ref.1, bf16[2,64,512]{2,1,0:T(8,128)(2,1)} %bitcast.2, bf16[2,32,512]{2,1,0:T(8,128)(2,1)} %bitcast.3, bf16[2,64,2048]{2,1,0:T(8,128)(2,1)} %q_ref.1, s32[4]{0:T(128)} %se_ref.1), custom_call_target="tpu_custom_call" | custom-call | tf_op jit(solution)/shard_map/pallas_call | solution.py:536
  134.2 1.2 copy.9

commit v3 on v2

--- a/solution.py
+++ b/solution.py
@@ -9,9 +9,9 @@
 
 EXAMPLES = 2
 ROWS = 32
-TOP_ROUTED = (0, 0)
-LOW_ROUTED = (0, 0)
-LAGS = ((0, 0, 1, 2), (0, 1, 2, 3), (1, 2, 3, 4), (0, 1, 1, 1))
+TOP_ROUTED = (4, 11)
+DIRECT = (11, 16)
+LAGS = ((0, 0, 2, 3), (0, 1, 2, 3), (1, 2, 3, 4), (0, 1, 1, 1))
 MESH = pl.DeviceIdType.MESH
 NT = (((1,), (1,)), ((), ()))
 NN = (((1,), (0,)), ((), ()))
@@ -45,18 +45,23 @@
     has_lower = sec > 0
     pair_lower = lax.rem(sec, 2) == 1
     pair_upper = jnp.logical_not(pair_lower)
-    relays = sorted({(sections - 1, sections - 4), (3, 0)}) if sections >= 4 else []
+    helper = sections - 4
+
+    def scaled(span):
+        return [part * micro // 16 for part in span]
 
     def in_span(m, span):
-        return jnp.logical_and(m >= span[0], m < span[1])
+        low, high = scaled(span)
+        return jnp.logical_and(m >= low, m < high)
 
     def top_routed(m):
-        return in_span(m, TOP_ROUTED if relays else (0, 0))
-
-    def low_routed(m):
-        return in_span(m, LOW_ROUTED if relays else (0, 0))
+        return in_span(m, TOP_ROUTED if helper >= 0 else (0, 0))
+
+    def direct(m):
+        return in_span(m, DIRECT)
 
     far_fed = jnp.logical_and(pair_lower, jnp.logical_not(is_top))
+    far_lower = jnp.logical_and(pair_upper, has_lower)
 
     far = [z]
     for k in range(nz - 1):
@@ -131,14 +136,23 @@
     for step in range(1, sections):
         greet(lax.rem(sec + step, sections), tp)
     linked = 0
-    for pair in relays:
-        for here, there in (pair, pair[::-1]):
+    for when, there in ((far_fed, sec + 1), (far_lower, sec - 1)):
+        @pl.when(when)
+        def _(there=there):
+            for step in range(1, nz):
+                greet(there, peer_z(step))
+            for step in range(1, ny):
+                greet(there, peer_y(step))
+
+        linked = linked + (nz + ny - 2) * when.astype(jnp.int32)
+    if helper >= 0:
+        for here, there in ((sections - 1, helper), (helper, sections - 1)):
             @pl.when(sec == here)
             def _(there=there):
                 for step in range(1, tp_count):
                     greet(there, lax.rem(tp + step, tp_count))
 
-            linked = linked + (sec == here).astype(jnp.int32)
+            linked = linked + (tp_count - 1) * (sec == here).astype(jnp.int32)
 
     def turn_weights(layer):
         w_copy(layer).wait()
@@ -155,7 +169,7 @@
     def _():
         turn_weights(0)
 
-    pl.semaphore_wait(barrier, tp_count + nz + ny + sections - 4 + (tp_count - 1) * linked)
+    pl.semaphore_wait(barrier, tp_count + nz + ny + sections - 4 + linked)
 
     def slots(buf, m, count, ssem, rsem):
         part = buf.at[m, pl.ds(0, count)]
@@ -163,8 +177,9 @@
 
     def relay_copy(buf, sends, recvs, m, zstep, ystep):
         src = src_at(zstep, 0)
+        line = ny - ystep - (0 if zstep else 1)
         return remote(buf.at[m, src], buf.at[m, src], sends.at[m],
-                      recvs.at[m, ny - ystep], sec, peer_y(ystep))
+                      recvs.at[m, line], sec, peer_y(ystep))
 
     def forward_copy(buf, sends, recvs, m, ystep):
         src = src_at(0, ystep)
@@ -182,7 +197,7 @@
                       sec - 1, peer_z(zstep))
 
     def lower_y_copy(m, ystep):
-        return remote(buf_l.at[m], buf_u.at[m, tp], send_l.at[m], near_u.at[m, ny - ystep],
+        return remote(buf_l.at[m], buf_u.at[m, tp], send_l.at[m], near_u.at[m, ny - ystep - 1],
                       sec - 1, peer_y(ystep))
 
     def await_own(m):
@@ -192,7 +207,7 @@
         slots(buf, m, nz - 1, send_my, recvs.at[m, ystep]).wait_recv()
 
     def await_near(buf, nears, m, ystep):
-        slots(buf, m, 1, send_my, nears.at[m, ystep]).wait_recv()
+        slots(buf, m, 1, send_my, nears.at[m, ystep - 1]).wait_recv()
 
     def pass_on(buf, sends, recvs, nears, m):
         for ystep in range(1, ny):
@@ -208,8 +223,9 @@
         for zstep in [*range(nz - 1, 0, -1), 0]:
             for ystep in range(ny):
                 if zstep or ystep:
-                    sem = recvs if zstep else nears
-                    remote(buf_v.at[m], buf.at[m, tp], send_v.at[m], sem.at[m, (ny - ystep) % ny],
+                    line = (ny - ystep) % ny
+                    sem = recvs.at[m, line] if zstep else nears.at[m, line - 1]
+                    remote(buf_v.at[m], buf.at[m, tp], send_v.at[m], sem,
                            target, src_at(zstep, ystep)).start()
 
     def product(buf, m, layer, ystep, total=None):
@@ -226,13 +242,6 @@
         own = buf_u[m, tp]
         floats = own.astype(jnp.float32)
         slope = slope_of(h_ref[1, at, :])
-
-        @pl.when(jnp.logical_and(sec == 0, low_routed(m)))
-        def _():
-            await_line(buf_u, recv_u, m, 0)
-            for ystep in range(1, ny):
-                await_near(buf_u, near_u, m, ystep)
-
         total = product(buf_u, m, 1, 0)
         for ystep in range(1, ny):
             @pl.when(jnp.logical_not(is_top))
@@ -252,11 +261,11 @@
             for step in range(1, ny):
                 relay_copy(buf_m, send_m, near_m, m, 0, step).start()
 
-        if relays:
+        if helper >= 0:
             @pl.when(routed)
             def _():
                 remote(buf_m.at[m, tp], buf_v.at[m], send_m.at[m], recv_v.at[m],
-                       sections - 4, tp).start()
+                       helper, tp).start()
 
         feats = lax.dot_general(
             own, ob_v[1], NT, preferred_element_type=jnp.float32
@@ -283,41 +292,34 @@
             total = product(buf_m, m, 0, ystep, total)
         buf_l[m] = (floats + slope * total).astype(jnp.bfloat16)
 
-        routed = jnp.logical_and(sec == 1, low_routed(m))
-
-        @pl.when(jnp.logical_and(pair_lower, jnp.logical_not(routed)))
+        @pl.when(jnp.logical_or(pair_lower, direct(m)))
         def _():
             for step in range(1, nz):
                 lower_z_copy(m, step).start()
             for step in range(1, ny):
                 lower_y_copy(m, step).start()
 
-        if relays:
-            @pl.when(routed)
-            def _():
-                remote(buf_l.at[m], buf_v.at[m], send_l.at[m], recv_v.at[m], 3, tp).start()
-
         lower_own_copy(m).start()
 
     def tp_copy(src, dst, ssem, rsem, to_tp):
         return remote(src, dst, ssem, rsem, sec, to_tp)
 
-    def part_copy(step):
-        to = lax.rem(tp + step, tp_count)
-        return tp_copy(part_in.at[to], got_in.at[tp], part_send.at[step], part_recv.at[tp], to)
-
-    def full_copy(step):
-        to = lax.rem(tp + step, tp_count)
-        return tp_copy(full_in.at[tp], full_in.at[tp], full_send.at[step], full_recv.at[tp], to)
-
-    def grad_copy(step):
-        to = lax.rem(tp + step, tp_count)
-        return tp_copy(grad_v.at[tp], grad_v.at[tp], grad_send.at[step], grad_recv.at[tp], to)
+    others = [(zstep, ystep) for zstep in [*range(nz - 1, 0, -1), 0]
+              for ystep in range(ny) if zstep or ystep]
+
+    def share(src_of, dst_ref, ssem, rsem):
+        for zstep, ystep in others:
+            to = src_at(zstep, ystep)
+            tp_copy(src_of(to), dst_ref, ssem, rsem, to).start()
+
+    def shared(buf, ssem, rsem):
+        part = buf.at[pl.ds(0, tp_count - 1)]
+        return tp_copy(part, part, ssem, rsem, tp)
 
     def score_copy(step):
         to = lax.rem(sec + step, sections)
-        return remote(score_v.at[sec], score_v.at[sec], score_send.at[step],
-                      score_recv.at[sec], to, tp)
+        return remote(score_v.at[sec], score_v.at[sec], score_send,
+                      score_recv, to, tp)
 
     def project_inputs():
         part_rows = part_in.shape[1]
@@ -334,16 +336,13 @@
                 total = term if total is None else total + term
             part_in[k] = total
 
+        share(lambda to: part_in.at[to], got_in.at[tp], part_send, part_recv)
+        total = part_in[tp]
+        shared(got_in, send_my, part_recv).wait_recv()
         for step in range(1, tp_count):
-            part_copy(step).start()
-        total = part_in[tp]
-        for step in range(1, tp_count):
-            src = lax.rem(tp + step, tp_count)
-            tp_copy(got_in.at[src], got_in.at[src], send_my, part_recv.at[src], tp).wait_recv()
-            total = total + got_in[src]
+            total = total + got_in[lax.rem(tp + step, tp_count)]
         full_in[tp] = total
-        for step in range(1, tp_count):
-            full_copy(step).start()
+        share(lambda to: full_in.at[tp], full_in.at[tp], full_send, full_recv)
 
     @pl.when(sec < sections // 2)
     def _():
@@ -357,13 +356,11 @@
             relay_copy(buf_u, send_u, near_u, m, 0, step).start()
 
     def pass_upper(m):
-        @pl.when(pair_upper)
+        @pl.when(jnp.logical_or(pair_upper, direct(m)))
         def _():
             await_own(m)
 
-        @pl.when(jnp.logical_not(jnp.logical_and(sec == 0, low_routed(m))))
-        def _():
-            pass_on(buf_u, send_u, recv_u, near_u, m)
+        pass_on(buf_u, send_u, recv_u, near_u, m)
 
     def pass_middle(m):
         @pl.when(jnp.logical_not(jnp.logical_and(is_top, top_routed(m))))
@@ -384,10 +381,10 @@
     lag_pass, lag_upper, lag_middle, lag_lower = [lag_of(k) for k in range(4)]
     steps = micro + max(max(lags) for lags in LAGS)
 
-    if relays:
-        @pl.when(sec == sections - 4)
-        def _():
-            @pl.loop(*TOP_ROUTED)
+    if helper >= 0:
+        @pl.when(sec == helper)
+        def _():
+            @pl.loop(*scaled(TOP_ROUTED))
             def _(m):
                 routed_on(buf_m, recv_m, near_m, m, sections - 1)
 
@@ -398,7 +395,7 @@
         m_mid = it - lag_middle
         m_low = it - lag_lower
 
-        @pl.when(jnp.logical_and(it < micro, far_fed))
+        @pl.when(jnp.logical_and(jnp.logical_and(it < micro, far_fed), jnp.logical_not(direct(it))))
         def _():
             spread_upper(it)
 
@@ -431,16 +428,7 @@
     def _():
         project_inputs()
 
-    if relays:
-        @pl.when(sec == 3)
-        def _():
-            @pl.loop(*LOW_ROUTED)
-            def _(m):
-                routed_on(buf_u, recv_u, near_u, m, 0)
-
-    for step in range(1, tp_count):
-        src = lax.rem(tp + step, tp_count)
-        tp_copy(full_in.at[src], full_in.at[src], send_my, full_recv.at[src], tp).wait_recv()
+    shared(full_in, send_my, full_recv).wait_recv()
     lanes = 2 * rank_in
     pairs = EXAMPLES * rank_out
     product_all = lax.dot_general(
@@ -449,11 +437,8 @@
     lane = lax.broadcasted_iota(jnp.int32, (pairs, lanes), 1)
     own_grad = jnp.where(lane < rank_in, product_all[:pairs], product_all[pairs:])
     grad_v[tp] = own_grad.astype(jnp.bfloat16)
-    for step in range(1, tp_count):
-        grad_copy(step).start()
-    for step in range(1, tp_count):
-        src = lax.rem(tp + step, tp_count)
-        tp_copy(grad_v.at[src], grad_v.at[src], send_my, grad_recv.at[src], tp).wait_recv()
+    share(lambda to: grad_v.at[tp], grad_v.at[tp], grad_send, grad_recv)
+    shared(grad_v, send_my, grad_recv).wait_recv()
     total = grad_v[0].astype(jnp.float32)
     for k in range(1, tp_count):
         total = total + grad_v[k].astype(jnp.float32)
@@ -477,21 +462,18 @@
         precision=lax.Precision.HIGHEST, preferred_element_type=jnp.float32)
     for step in range(1, sections):
         score_copy(step).start()
-    for step in range(1, sections):
-        src = lax.rem(sec + step, sections)
-        remote(score_v.at[src], score_v.at[src], send_my, score_recv.at[src], sec, tp).wait_recv()
+    scores = score_v.at[pl.ds(0, sections - 1)]
+    remote(scores, scores, send_my, score_recv, sec, tp).wait_recv()
     total = score_v[0]
     for k in range(1, sections):
         total = total + score_v[k]
     for example in range(EXAMPLES):
         score_ref[example:example + 1, :] = total[0:1, example * number:(example + 1) * number]
 
-    for step in range(1, tp_count):
-        part_copy(step).wait_send()
-        full_copy(step).wait_send()
-        grad_copy(step).wait_send()
-    for step in range(1, sections):
-        score_copy(step).wait_send()
+    shared(part_in, part_send, send_my).wait_send()
+    shared(full_in, full_send, send_my).wait_send()
+    shared(grad_v, grad_send, send_my).wait_send()
+    remote(scores, scores, score_send, send_my, sec, tp).wait_send()
 
     def sent(sends, buf, m, count, when):
         @pl.when(when)
@@ -501,20 +483,19 @@
     @pl.loop(0, micro)
     def _(m):
         top_far = jnp.logical_and(is_top, top_routed(m))
-        low_far = jnp.logical_and(sec == 1, low_routed(m))
-        in_far = jnp.logical_and(sec == 0, low_routed(m))
-        sent(send_u, buf_u, m, tp_count - 1, far_fed)
-        sent(send_u, buf_u, m, (nz - 1) * (ny - 1),
-             jnp.logical_and(jnp.logical_and(pair_upper, ny > 1), jnp.logical_not(in_far)))
+        spread = jnp.logical_and(far_fed, jnp.logical_not(direct(m)))
+        hop = jnp.logical_and(far_lower, jnp.logical_not(direct(m)))
+        sent(send_u, buf_u, m, tp_count - 1, spread)
+        if ny > 1:
+            sent(send_u, buf_u, m, (nz - 1) * (ny - 1),
+                 jnp.logical_not(jnp.logical_or(is_top, spread)))
         sent(send_m, buf_m, m, tp_count - 1, jnp.logical_and(has_lower, jnp.logical_not(top_far)))
         sent(send_m, buf_m, m, 1, top_far)
-        sent(send_l, buf_u, m, nz + ny - 1, jnp.logical_and(pair_lower, jnp.logical_not(low_far)))
-        sent(send_l, buf_u, m, 2, low_far)
-        sent(send_l, buf_u, m, 1, jnp.logical_and(pair_upper, has_lower))
-        if relays:
-            sent(send_v, buf_u, m, tp_count - 1, jnp.logical_or(
-                jnp.logical_and(sec == sections - 4, top_routed(m)),
-                jnp.logical_and(sec == 3, low_routed(m))))
+        sent(send_l, buf_u, m, nz + ny - 1, jnp.logical_and(has_lower, jnp.logical_not(hop)))
+        sent(send_l, buf_u, m, 1, hop)
+        if helper >= 0:
+            sent(send_v, buf_u, m, tp_count - 1,
+                 jnp.logical_and(sec == helper, top_routed(m)))
 
 
 def shards(
@@ -559,22 +540,22 @@
             dma((micro,)),
             dma((micro, ny)),
             dma((micro, ny)),
-            dma((micro, ny)),
-            dma((micro, ny)),
-            dma((micro,)),
-            dma((micro,)),
-            dma((micro,)),
-            dma((micro,)),
-            dma((micro,)),
-            dma,
-            dma((tp_count,)),
-            dma((tp_count,)),
-            dma((tp_count,)),
-            dma((tp_count,)),
-            dma((tp_count,)),
-            dma((tp_count,)),
-            dma((sections,)),
-            dma((sections,)),
+            dma((micro, max(ny - 1, 1))),
+            dma((micro, max(ny - 1, 1))),
+            dma((micro,)),
+            dma((micro,)),
+            dma((micro,)),
+            dma((micro,)),
+            dma((micro,)),
+            dma,
+            dma,
+            dma,
+            dma,
+            dma,
+            dma,
+            dma,
+            dma,
+            dma,
         ],
         compiler_params=pltpu.CompilerParams(
             collective_id=0, has_side_effects=True, vmem_limit_bytes=56 * 2**20),

time: 136 us -> 129 us (0.949)
  Pallas kernels: 134 us -> 127 us
    pallas_call x1, Pallas kernels: 134 us -> 127 us  [shards(): pl.pallas_call(functools.partial(chain_kernel, sections, tp_count), out_s...]
where the time goes in v3:
time: 129 us; the launch traced here: 128 us
  Pallas kernels  127 us (98%)
    pallas_call x1, Pallas kernels, shards(): pl.pallas_call(functools.partial(chain_kernel, sections, tp_count), out_s...  127 us

profile of v3, /device:TPU:0, one launch (start us, length us, event | category | flops | bytes accessed | tf_op | source)
XLA Modules:
  0.0 128.4 jit_solution(3376914448682567902)
XLA Ops:
  0.0 127.2 %shard_map.73 = f32[2,64]{1,0:T(2,128)} custom-call(bf16[512,4096]{1,0:T(8,128)(2,1)} %top_ref.1, bf16[2,512,4096]{2,1,0:T(8,128)(2,1)} %w_ref.1, bf16[2,512,512]{2,1,0:T(8,128)(2,1)} %h_ref.1, bf16[2,64,512]{2,1,0:T(8,128)(2,1)} %bitcast.2, bf16[2,32,512]{2,1,0:T(8,128)(2,1)} %bitcast.3, bf16[2,64,2048]{2,1,0:T(8,128)(2,1)} %q_ref.1, s32[4]{0:T(128)} %se_ref.1), custom_call_target="tpu_custom_call" | custom-call | tf_op jit(solution)/shard_map/pallas_call | solution.py:517
  127.2 1.2 copy.9

commit v4 on v3

--- a/solution.py
+++ b/solution.py
@@ -218,15 +218,11 @@
             for ystep in range(1, ny):
                 relay_copy(buf, sends, recvs, m, zstep, ystep).start()
 
-    def routed_on(buf, recvs, nears, m, target):
+    def routed_on(buf, recvs, m, target):
         remote(buf_v.at[m], buf_v.at[m], send_my, recv_v.at[m], sec, tp).wait_recv()
-        for zstep in [*range(nz - 1, 0, -1), 0]:
-            for ystep in range(ny):
-                if zstep or ystep:
-                    line = (ny - ystep) % ny
-                    sem = recvs.at[m, line] if zstep else nears.at[m, line - 1]
-                    remote(buf_v.at[m], buf.at[m, tp], send_v.at[m], sem,
-                           target, src_at(zstep, ystep)).start()
+        for zstep in range(nz - 1, 0, -1):
+            remote(buf_v.at[m], buf.at[m, tp], send_v.at[m], recvs.at[m, 0],
+                   target, src_at(zstep, 0)).start()
 
     def product(buf, m, layer, ystep, total=None):
         for zstep in range(nz):
@@ -258,6 +254,9 @@
         def _():
             for step in range(1, nz):
                 spread_copy(buf_m, send_m, recv_m, m, step).start()
+
+        @pl.when(has_lower)
+        def _():
             for step in range(1, ny):
                 relay_copy(buf_m, send_m, near_m, m, 0, step).start()
 
@@ -279,12 +278,6 @@
         at = pl.ds(pl.multiple_of(m * rows, rows), rows)
         floats = buf_m[m, tp].astype(jnp.float32)
         slope = slope_of(h_ref[0, at, :])
-
-        @pl.when(jnp.logical_and(is_top, top_routed(m)))
-        def _():
-            await_line(buf_m, recv_m, m, 0)
-            for ystep in range(1, ny):
-                await_near(buf_m, near_m, m, ystep)
 
         total = product(buf_m, m, 0, 0)
         for ystep in range(1, ny):
@@ -363,9 +356,7 @@
         pass_on(buf_u, send_u, recv_u, near_u, m)
 
     def pass_middle(m):
-        @pl.when(jnp.logical_not(jnp.logical_and(is_top, top_routed(m))))
-        def _():
-            pass_on(buf_m, send_m, recv_m, near_m, m)
+        pass_on(buf_m, send_m, recv_m, near_m, m)
 
     def within(m):
         return jnp.logical_and(m >= 0, m < micro)
@@ -386,7 +377,7 @@
         def _():
             @pl.loop(*scaled(TOP_ROUTED))
             def _(m):
-                routed_on(buf_m, recv_m, near_m, m, sections - 1)
+                routed_on(buf_m, recv_m, m, sections - 1)
 
     @pl.loop(0, steps)
     def _(it):
@@ -490,11 +481,11 @@
             sent(send_u, buf_u, m, (nz - 1) * (ny - 1),
                  jnp.logical_not(jnp.logical_or(is_top, spread)))
         sent(send_m, buf_m, m, tp_count - 1, jnp.logical_and(has_lower, jnp.logical_not(top_far)))
-        sent(send_m, buf_m, m, 1, top_far)
+        sent(send_m, buf_m, m, 1 + nz * (ny - 1), top_far)
         sent(send_l, buf_u, m, nz + ny - 1, jnp.logical_and(has_lower, jnp.logical_not(hop)))
         sent(send_l, buf_u, m, 1, hop)
         if helper >= 0:
-            sent(send_v, buf_u, m, tp_count - 1,
+            sent(send_v, buf_u, m, nz - 1,
                  jnp.logical_and(sec == helper, top_routed(m)))
 
 

time: 129 us -> 127 us (0.984)
    pallas_call x1, Pallas kernels: 127 us -> 126 us  [shards(): pl.pallas_call(functools.partial(chain_kernel, sections, tp_count), out_s...]
where the time goes in v4:
time: 127 us
  Pallas kernels  126 us (99%)
    pallas_call x1, Pallas kernels, shards(): pl.pallas_call(functools.partial(chain_kernel, sections, tp_count), out_s...  126 us

profile of v4, /device:TPU:0, one launch (start us, length us, event | category | flops | bytes accessed | tf_op | source)
XLA Modules:
  0.0 126.9 jit_solution(6413794851009664718)
XLA Ops:
  0.0 125.6 %shard_map.73 = f32[2,64]{1,0:T(2,128)} custom-call(bf16[512,4096]{1,0:T(8,128)(2,1)} %top_ref.1, bf16[2,512,4096]{2,1,0:T(8,128)(2,1)} %w_ref.1, bf16[2,512,512]{2,1,0:T(8,128)(2,1)} %h_ref.1, bf16[2,64,512]{2,1,0:T(8,128)(2,1)} %bitcast.2, bf16[2,32,512]{2,1,0:T(8,128)(2,1)} %bitcast.3, bf16[2,64,2048]{2,1,0:T(8,128)(2,1)} %q_ref.1, s32[4]{0:T(128)} %se_ref.1), custom_call_target="tpu_custom_call" | custom-call | tf_op jit(solution)/shard_map/pallas_call | solution.py:508
  125.6 1.2 copy.9

commit v5 on v4

--- a/solution.py
+++ b/solution.py
@@ -9,7 +9,7 @@
 
 EXAMPLES = 2
 ROWS = 32
-TOP_ROUTED = (4, 11)
+TOP_ROUTED = (4, 12)
 DIRECT = (11, 16)
 LAGS = ((0, 0, 2, 3), (0, 1, 2, 3), (1, 2, 3, 4), (0, 1, 1, 1))
 MESH = pl.DeviceIdType.MESH
@@ -453,18 +453,9 @@
         precision=lax.Precision.HIGHEST, preferred_element_type=jnp.float32)
     for step in range(1, sections):
         score_copy(step).start()
-    scores = score_v.at[pl.ds(0, sections - 1)]
-    remote(scores, scores, send_my, score_recv, sec, tp).wait_recv()
-    total = score_v[0]
-    for k in range(1, sections):
-        total = total + score_v[k]
-    for example in range(EXAMPLES):
-        score_ref[example:example + 1, :] = total[0:1, example * number:(example + 1) * number]
-
     shared(part_in, part_send, send_my).wait_send()
     shared(full_in, full_send, send_my).wait_send()
     shared(grad_v, grad_send, send_my).wait_send()
-    remote(scores, scores, score_send, send_my, sec, tp).wait_send()
 
     def sent(sends, buf, m, count, when):
         @pl.when(when)
@@ -487,6 +478,15 @@
         if helper >= 0:
             sent(send_v, buf_u, m, nz - 1,
                  jnp.logical_and(sec == helper, top_routed(m)))
+
+    scores = score_v.at[pl.ds(0, sections - 1)]
+    remote(scores, scores, send_my, score_recv, sec, tp).wait_recv()
+    total = score_v[0]
+    for k in range(1, sections):
+        total = total + score_v[k]
+    for example in range(EXAMPLES):
+        score_ref[example:example + 1, :] = total[0:1, example * number:(example + 1) * number]
+    remote(scores, scores, score_send, send_my, sec, tp).wait_send()
 
 
 def shards(

time: 127 us -> 126 us (level)
  no operation moved by 1% of the time
where the time goes in v5:
time: 126 us
  Pallas kernels  125 us (99%)
    pallas_call x1, Pallas kernels, shards(): pl.pallas_call(functools.partial(chain_kernel, sections, tp_count), out_s...  125 us

profile of v5, /device:TPU:0, one launch (start us, length us, event | category | flops | bytes accessed | tf_op | source)
XLA Modules:
  0.0 125.8 jit_solution(4199374634943313809)
XLA Ops:
  0.0 124.6 %shard_map.73 = f32[2,64]{1,0:T(2,128)} custom-call(bf16[512,4096]{1,0:T(8,128)(2,1)} %top_ref.1, bf16[2,512,4096]{2,1,0:T(8,128)(2,1)} %w_ref.1, bf16[2,512,512]{2,1,0:T(8,128)(2,1)} %h_ref.1, bf16[2,64,512]{2,1,0:T(8,128)(2,1)} %bitcast.2, bf16[2,32,512]{2,1,0:T(8,128)(2,1)} %bitcast.3, bf16[2,64,2048]{2,1,0:T(8,128)(2,1)} %q_ref.1, s32[4]{0:T(128)} %se_ref.1), custom_call_target="tpu_custom_call" | custom-call | tf_op jit(solution)/shard_map/pallas_call | solution.py:508
  124.6 1.2 copy.9

commit v6 on v5

--- a/solution.py
+++ b/solution.py
@@ -9,7 +9,7 @@
 
 EXAMPLES = 2
 ROWS = 32
-TOP_ROUTED = (4, 12)
+TOP_ROUTED = (5, 13)
 DIRECT = (11, 16)
 LAGS = ((0, 0, 2, 3), (0, 1, 2, 3), (1, 2, 3, 4), (0, 1, 1, 1))
 MESH = pl.DeviceIdType.MESH

time: 126 us -> 125 us (level)
  no operation moved by 1% of the time
where the time goes in v6:
time: 125 us
  Pallas kernels  124 us (99%)
    pallas_call x1, Pallas kernels, shards(): pl.pallas_call(functools.partial(chain_kernel, sections, tp_count), out_s...  124 us

profile of v6, /device:TPU:0, one launch (start us, length us, event | category | flops | bytes accessed | tf_op | source)
XLA Modules:
  0.0 125.2 jit_solution(16326505614422281002)
XLA Ops:
  0.0 124.0 %shard_map.73 = f32[2,64]{1,0:T(2,128)} custom-call(bf16[512,4096]{1,0:T(8,128)(2,1)} %top_ref.1, bf16[2,512,4096]{2,1,0:T(8,128)(2,1)} %w_ref.1, bf16[2,512,512]{2,1,0:T(8,128)(2,1)} %h_ref.1, bf16[2,64,512]{2,1,0:T(8,128)(2,1)} %bitcast.2, bf16[2,32,512]{2,1,0:T(8,128)(2,1)} %bitcast.3, bf16[2,64,2048]{2,1,0:T(8,128)(2,1)} %q_ref.1, s32[4]{0:T(128)} %se_ref.1), custom_call_target="tpu_custom_call" | custom-call | tf_op jit(solution)/shard_map/pallas_call | solution.py:508
  124.0 1.2 copy.9

commit v7 on v6

--- a/solution.py
+++ b/solution.py
@@ -9,7 +9,7 @@
 
 EXAMPLES = 2
 ROWS = 32
-TOP_ROUTED = (5, 13)
+TOP_ROUTED = (6, 14)
 DIRECT = (11, 16)
 LAGS = ((0, 0, 2, 3), (0, 1, 2, 3), (1, 2, 3, 4), (0, 1, 1, 1))
 MESH = pl.DeviceIdType.MESH

time: 125 us -> 126 us (level)
  no operation moved by 1% of the time
where the time goes in v7:
time: 126 us
  Pallas kernels  125 us (99%)
    pallas_call x1, Pallas kernels, shards(): pl.pallas_call(functools.partial(chain_kernel, sections, tp_count), out_s...  125 us

profile of v7, /device:TPU:0, one launch (start us, length us, event | category | flops | bytes accessed | tf_op | source)
XLA Modules:
  0.0 125.9 jit_solution(8035694396848145604)
XLA Ops:
  0.0 124.7 %shard_map.73 = f32[2,64]{1,0:T(2,128)} custom-call(bf16[512,4096]{1,0:T(8,128)(2,1)} %top_ref.1, bf16[2,512,4096]{2,1,0:T(8,128)(2,1)} %w_ref.1, bf16[2,512,512]{2,1,0:T(8,128)(2,1)} %h_ref.1, bf16[2,64,512]{2,1,0:T(8,128)(2,1)} %bitcast.2, bf16[2,32,512]{2,1,0:T(8,128)(2,1)} %bitcast.3, bf16[2,64,2048]{2,1,0:T(8,128)(2,1)} %q_ref.1, s32[4]{0:T(128)} %se_ref.1), custom_call_target="tpu_custom_call" | custom-call | tf_op jit(solution)/shard_map/pallas_call | solution.py:508
  124.7 1.2 copy.9
